TPU v7x, 32 devices: a whole 2x2x4 slice. The times are simulated.
32 devices in a mesh: dp: 16 (over z, x, core), mp: 2 (over y).
Axes of the slice: x: 2, y: 2, z: 4, core: 2. Of those that a mesh axis runs over, the one named last changes fastest.
Arguments:
- tokens: bfloat16 [16384, 1024], P('dp'), may hold values from -6 to 6
- page_lengths: int32 [32], P('dp'), may hold values from 64 to 512, as said below
- qkv_weight: bfloat16 [3, 1024, 1024], P(None, None, 'mp'), may hold values from -0.1875 to 0.1875
- qv_bias: bfloat16 [2, 1024], P(None, 'mp'), may hold values from -1.5 to 1.5
- out_weight: bfloat16 [1024, 1024], P('mp'), may hold values from -0.75 to 0.75
- out_bias: bfloat16 [1024], replicated, may hold values from -1.5 to 1.5
- ln1_gain: bfloat16 [1024], replicated, may hold values from 0.5 to 1.5
- ln1_bias: bfloat16 [1024], replicated, may hold values from -1.5 to 1.5
- ff1_weight: bfloat16 [1024, 4096], P(None, 'mp'), may hold values from -0.1875 to 0.1875
- ff1_bias: bfloat16 [4096], P('mp'), may hold values from -1.5 to 1.5
- ff2_weight: bfloat16 [4096, 1024], P('mp'), may hold values from -0.09375 to 0.09375
- ff2_bias: bfloat16 [1024], replicated, may hold values from -1.5 to 1.5
- ln2_gain: bfloat16 [1024], replicated, may hold values from 0.5 to 1.5
- ln2_bias: bfloat16 [1024], replicated, may hold values from -1.5 to 1.5
- cotangent: bfloat16 [16384, 1024], P('dp'), may hold values from -6 to 6
Outputs:
- out_rows: bfloat16 [16384, 1024], P(('dp', 'mp'))
- input_grad: bfloat16 [16384, 1024], P(('dp', 'mp'))
- qkv_weight_grad: float32 [3, 1024, 1024], P(None, 'dp', 'mp')
- qv_bias_grad: float32 [2, 1024], replicated
- out_weight_grad: float32 [1024, 1024], P('mp', 'dp')
- out_bias_grad: float32 [1024], replicated
- ln1_gain_grad: float32 [1024], replicated
- ln1_bias_grad: float32 [1024], replicated
- ff1_weight_grad: float32 [1024, 4096], P('dp', 'mp')
- ff1_bias_grad: float32 [4096], replicated
- ff2_weight_grad: float32 [4096, 1024], P('mp', 'dp')
- ff2_bias_grad: float32 [1024], replicated
- ln2_gain_grad: float32 [1024], replicated
- ln2_bias_grad: float32 [1024], replicated
Inputs may be any that keep to these rules, and one draw needn't show every extreme that they name: `page_lengths`: valid tokens of a page; some page has all 512 slots valid.
All inputs are finite; a program needn't handle non-finite values.
Results may differ from a plain program's by a relative error of at most 0.02.
Values may be sent and summed in bfloat16 or wider, within the bound.
No kernel may reach another device: no remote copies, remote signals or barrier semaphores. Data moves between devices by JAX's collectives and lax.ppermute only.
A program may use at most 192 MiB of HBM per device.

v0:
```python
import jax
import jax.numpy as jnp
from jax import lax
from jax.sharding import PartitionSpec as P

HD = 64
EPSILON = 1e-05
NEGATIVE = -1e30


def normalize(values):
    center = values - jnp.mean(values, axis=-1, keepdims=True)
    spread = jnp.mean(center * center, axis=-1, keepdims=True)
    return center * lax.rsqrt(spread + EPSILON)


def gelu_exact(values):
    return jax.nn.gelu(values, approximate=False)


def over_rows(left, right):
    return lax.dot_general(
        left, right, (((0,), (0,)), ((), ())), preferred_element_type=jnp.float32
    )


def over_cols(left, right):
    return lax.dot_general(
        left, right, (((1,), (1,)), ((), ())), preferred_element_type=jnp.float32
    )


def page_scores(query, keyset, valid):
    raw = jnp.einsum("qhe,khe->hqk", query, keyset, preferred_element_type=jnp.float32) * HD ** (
        -0.5
    )
    return jnp.where(valid[None, None, :], raw, NEGATIVE)


def attend(block):
    query, keyset, valueset, valid = block
    scores = page_scores(query, keyset, valid)
    top = jnp.max(scores, axis=-1, keepdims=True)
    expo = jnp.exp(scores - top)
    total = jnp.sum(expo, axis=-1, keepdims=True)
    probs = expo / total
    context = jnp.einsum(
        "hqk,khe->qhe", probs.astype(jnp.bfloat16), valueset, preferred_element_type=jnp.float32
    )
    context = context.astype(jnp.bfloat16)
    return (context.reshape(context.shape[0], -1), top[..., 0] + jnp.log(total[..., 0]))


def attend_back(block):
    query, keyset, valueset, valid, logsum, dcontext = block
    scale = HD ** (-0.5)
    scores = page_scores(query, keyset, valid)
    probs = jnp.exp(scores - logsum[..., None])
    dprobs = jnp.einsum("qhe,khe->hqk", dcontext, valueset, preferred_element_type=jnp.float32)
    delta = jnp.sum(probs * dprobs, axis=-1, keepdims=True)
    dscores = (probs * (dprobs - delta)).astype(jnp.bfloat16)
    dquery = (
        jnp.einsum("hqk,khe->qhe", dscores, keyset, preferred_element_type=jnp.float32) * scale
    ).astype(jnp.bfloat16)
    dkeys = (
        jnp.einsum("hqk,qhe->khe", dscores, query, preferred_element_type=jnp.float32) * scale
    ).astype(jnp.bfloat16)
    dvalues = jnp.einsum(
        "hqk,qhe->khe", probs.astype(jnp.bfloat16), dcontext, preferred_element_type=jnp.float32
    ).astype(jnp.bfloat16)
    seq_len = query.shape[0]
    return (dquery.reshape(seq_len, -1), dkeys.reshape(seq_len, -1), dvalues.reshape(seq_len, -1))


def local(
    tokens,
    page_lengths,
    qkv_weight,
    qv_bias,
    out_weight,
    out_bias,
    ln1_gain,
    ln1_bias,
    ff1_weight,
    ff1_bias,
    ff2_weight,
    ff2_bias,
    ln2_gain,
    ln2_bias,
    cotangent,
):
    row_count = tokens.shape[0]
    page_count = page_lengths.shape[0]
    seq_len = row_count // page_count
    cols = qkv_weight.shape[2]
    ff_cols = ff1_weight.shape[1]
    group_heads = cols // HD
    share = row_count // lax.axis_size("mp")
    group = lax.axis_index("mp")
    share_start = group * share
    gain_one = ln1_gain.astype(jnp.float32)
    shift_one = ln1_bias.astype(jnp.float32)
    gain_two = ln2_gain.astype(jnp.float32)
    shift_two = ln2_bias.astype(jnp.float32)

    def own_rows(values):
        return lax.dynamic_slice_in_dim(values, share_start, share, 0)

    projected = jnp.einsum("rd,tdc->trc", tokens, qkv_weight, preferred_element_type=jnp.float32)
    bias_rows = jnp.stack([qv_bias[0], jnp.zeros_like(qv_bias[0]), qv_bias[1]]).astype(jnp.float32)
    qkv_rows = (projected + bias_rows[:, None, :]).astype(jnp.bfloat16)
    qkv_pages = qkv_rows.reshape(3, page_count, seq_len, group_heads, HD)
    valid = jnp.arange(seq_len)[None, :] < page_lengths[:, None]
    context, logsum = lax.map(attend, (qkv_pages[0], qkv_pages[1], qkv_pages[2], valid))
    context = context.reshape(row_count, cols)
    attn_part = jnp.dot(context, out_weight, preferred_element_type=jnp.float32).astype(
        jnp.bfloat16
    )
    attn = lax.psum(attn_part, "mp").astype(jnp.float32)
    first_sum = tokens.astype(jnp.float32) + attn + out_bias.astype(jnp.float32)
    normed_one, norm_one_back = jax.vjp(normalize, first_sum)
    hidden = normed_one * gain_one + shift_one
    hidden_low = hidden.astype(jnp.bfloat16)
    normed_one_own = own_rows(normed_one)
    pre = jnp.dot(hidden_low, ff1_weight, preferred_element_type=jnp.float32) + ff1_bias.astype(
        jnp.float32
    )
    activated, gelu_back = jax.vjp(gelu_exact, pre)
    act_low = activated.astype(jnp.bfloat16)
    ffn_part = jnp.dot(act_low, ff2_weight, preferred_element_type=jnp.float32).astype(jnp.bfloat16)
    cot_own = own_rows(cotangent).astype(jnp.float32)
    ffn = lax.psum(ffn_part, "mp").astype(jnp.float32)
    second_sum = hidden + ffn + ff2_bias.astype(jnp.float32)
    normed_two, norm_two_back = jax.vjp(normalize, second_sum)
    normed_two_own = own_rows(normed_two)
    out_rows = (normed_two_own * gain_two + shift_two).astype(jnp.bfloat16)
    dsecond = norm_two_back(cotangent.astype(jnp.float32) * gain_two)[0]
    dffn = dsecond.astype(jnp.bfloat16)
    dsecond_own = own_rows(dsecond)
    dgain_two = jnp.sum(cot_own * normed_two_own, axis=0)
    dshift_two = jnp.sum(cot_own, axis=0)
    dff2_bias = jnp.sum(dsecond_own, axis=0)
    dff2_weight = over_rows(act_low, dffn)
    dact = over_cols(dffn, ff2_weight)
    dpre = gelu_back(dact)[0].astype(jnp.bfloat16)
    dff1_bias = jnp.sum(dpre.astype(jnp.float32), axis=0)
    dff1_weight = over_rows(hidden_low, dpre)
    dhid_part = over_cols(dpre, ff1_weight).astype(jnp.bfloat16)
    dhidden = dsecond + lax.psum(dhid_part, "mp").astype(jnp.float32)
    dfirst = norm_one_back(dhidden * gain_one)[0]
    dattn = dfirst.astype(jnp.bfloat16)
    dhidden_own = own_rows(dhidden)
    dfirst_own = own_rows(dfirst)
    dgain_one = jnp.sum(dhidden_own * normed_one_own, axis=0)
    dshift_one = jnp.sum(dhidden_own, axis=0)
    dout_bias = jnp.sum(dfirst_own, axis=0)
    dout_weight = over_rows(context, dattn)
    dcontext = over_cols(dattn, out_weight).astype(jnp.bfloat16)
    dcontext_pages = dcontext.reshape(page_count, seq_len, group_heads, HD)
    dquery, dkeys, dvalues = lax.map(
        attend_back, (qkv_pages[0], qkv_pages[1], qkv_pages[2], valid, logsum, dcontext_pages)
    )
    dqkv = jnp.stack(
        [
            dquery.reshape(row_count, cols),
            dkeys.reshape(row_count, cols),
            dvalues.reshape(row_count, cols),
        ]
    )
    dqv_bias = jnp.stack(
        [jnp.sum(dqkv[0].astype(jnp.float32), axis=0), jnp.sum(dqkv[2].astype(jnp.float32), axis=0)]
    )
    dqkv_weight = jnp.einsum("rd,trc->tdc", tokens, dqkv, preferred_element_type=jnp.float32)
    dtok_part = jnp.einsum(
        "trc,tdc->rd", dqkv, qkv_weight, preferred_element_type=jnp.float32
    ).astype(jnp.bfloat16)
    input_grad = (
        dfirst_own
        + lax.psum_scatter(dtok_part, "mp", scatter_dimension=0, tiled=True).astype(jnp.float32)
    ).astype(jnp.bfloat16)
    qkv_share, out_share, ff1_share, ff2_share = (
        lax.psum_scatter(
            dqkv_weight.astype(jnp.bfloat16), "dp", scatter_dimension=1, tiled=True
        ).astype(jnp.float32),
        lax.psum_scatter(
            dout_weight.astype(jnp.bfloat16), "dp", scatter_dimension=1, tiled=True
        ).astype(jnp.float32),
        lax.psum_scatter(
            dff1_weight.astype(jnp.bfloat16), "dp", scatter_dimension=0, tiled=True
        ).astype(jnp.float32),
        lax.psum_scatter(
            dff2_weight.astype(jnp.bfloat16), "dp", scatter_dimension=1, tiled=True
        ).astype(jnp.float32),
    )
    qv_placed = lax.dynamic_update_slice_in_dim(
        jnp.zeros((2, cols * lax.axis_size("mp")), jnp.float32), dqv_bias, group * cols, 1
    )
    ff1_placed = lax.dynamic_update_slice_in_dim(
        jnp.zeros((ff_cols * lax.axis_size("mp"),), jnp.float32), dff1_bias, group * ff_cols, 0
    )
    small = lax.psum(
        (qv_placed, dout_bias, dgain_one, dshift_one, ff1_placed, dff2_bias, dgain_two, dshift_two),
        ("dp", "mp"),
    )
    return (
        out_rows,
        input_grad,
        qkv_share,
        small[0],
        out_share,
        small[1],
        small[2],
        small[3],
        ff1_share,
        small[4],
        ff2_share,
        small[5],
        small[6],
        small[7],
    )


def solution(mesh):
    in_specs = (
        P("dp", None),
        P("dp"),
        P(None, None, "mp"),
        P(None, "mp"),
        P("mp", None),
        P(),
        P(),
        P(),
        P(None, "mp"),
        P("mp"),
        P("mp", None),
        P(),
        P(),
        P(),
        P("dp", None),
    )
    out_specs = (
        P(("dp", "mp"), None),
        P(("dp", "mp"), None),
        P(None, "dp", "mp"),
        P(),
        P("mp", "dp"),
        P(),
        P(),
        P(),
        P("dp", "mp"),
        P(),
        P("mp", "dp"),
        P(),
        P(),
        P(),
    )
    return jax.shard_map(local, mesh=mesh, in_specs=in_specs, out_specs=out_specs, check_vma=False)
```

profile of v0, /device:TPU:0, one launch (start us, length us, event | category | flops | bytes accessed | tf_op | source)
XLA Modules:
  0.0 775.8 jit_solution(8002461027185806768)
XLA Ops:
  9.1 5.5 fusion.56
  32.4 24.3 %while.26 = (s32[]{:T(128)}, bf16[2,512,512]{2,1,0:T(8,128)(2,1)}, f32[2,8,512]{2,1,0:T(8,128)S(1)}, bf16[2,512,8,64]{1,3,2,0:T(8,128)(2,1)}, pred[2,512]{1,0:T(...) while((s32[]{:T(128)}, bf16[2,512,512]{2,1,0:T(8,128)(2,1)}, ...), condition=%wide.region_3.4_spmd, body=%wide.region_0.3_spmd.sunk | while | flops 562294784 | bytes 33689224 | solution.py:114
  56.7 4.2 convolution_convert_fusion.4
  61.3 65.4 %all-reduce.7.cloned.1.call-done = bf16[1024,1024]{1,0:T(8,128)(2,1)} async-done(((bf16[1024,1024]{1,0:T(8,128)(2,1)}), bf16[1024,1024]{1,0:T(8,128)(2,1)}) %all-reduce.7.cloned.1.call-update) | async-done | bytes 2097168 | tf_op jit(solution)/shard_map/psum | solution.py:119
  133.5 24.4 %multiply_convert_fusion.1 = (bf16[1024,2048]{1,0:T(8,128)(2,1)S(1)}, f32[1024,2048]{1,0:T(8,128)}, f32[1024,2048]{1,0:T(8,128)}) fusion(f32[2048]{0:T(1024)S(1)} %convert_element_type.172, bf16[1024,2048]{1,0:T(8,128)(2,1)S(1)} %copy-done.36, f32[1024,1024]{1,0:T(8,128)S(1)} %broadcast_multiply_fusion, f32[1024]{0:T(1024)S(1)} %convert_element_type.170, ...), kind=kOutput, calls=%fused_computation.64 | convolution fusion | flops 4436525056 | bytes 29376512 | tf_op jit(solution)/shard_map/dot_general | solution.py:125
  159.9 5.7 convolution_convert_fusion.3
  166.2 62.6 %all-reduce.9.cloned.1.call-done = bf16[1024,1024]{1,0:T(8,128)(2,1)} async-done(((bf16[1024,1024]{1,0:T(8,128)(2,1)}), bf16[1024,1024]{1,0:T(8,128)(2,1)}) %all-reduce.9.cloned.1.call-update) | async-done | bytes 2097168 | tf_op jit(solution)/shard_map/psum | solution.py:132
  241.1 13.0 %convert_reduce_fusion = (f32[2048]{0:T(1024)}, bf16[1024,2048]{1,0:T(8,128)(2,1)}) fusion(f32[1024,2048]{1,0:T(8,128)} %get-tuple-element.258, bf16[2048,1024]{1,0:T(8,128)(2,1)S(1)} %copy-done.35, f32[1024,1024]{1,0:T(8,128)S(1)} %broadcast_add_fusion.1, f32[1024,2048]{1,0:T(8,128)} %get-tuple-element.275, f32[2048]{0:T(1024)S(1)} %convert_element_type.172), kind=kOutput, calls=%fused_computation.62 | convolution fusion | flops 4331665408 | bytes 29376512 | tf_op jit(solution)/shard_map/dot_general | solution.py:28
  254.1 8.0 %convolution_convert_fusion.2 = bf16[1024,1024]{1,0:T(8,128)(2,1)} fusion(bf16[1024,2048]{1,0:T(8,128)(2,1)} %get-tuple-element.277, bf16[1024,2048]{1,0:T(8,128)(2,1)S(1)} %copy-done.37), kind=kOutput, calls=%fused_computation.118 | convolution fusion | flops 4296015872 | bytes 10485760 | tf_op jit(solution)/shard_map/dot_general | solution.py:28
  262.2 63.0 %all-reduce.11.cloned.1.call-done = bf16[1024,1024]{1,0:T(8,128)(2,1)} async-done(((bf16[1024,1024]{1,0:T(8,128)(2,1)}), bf16[1024,1024]{1,0:T(8,128)(2,1)}) %all-reduce.11.cloned.1.call-update) | async-done | bytes 2097168 | tf_op jit(solution)/shard_map/psum | solution.py:149
  325.2 5.7 multiply_reduce_fusion.1
  346.2 42.9 %while.27 = (s32[]{:T(128)}, bf16[2,512,512]{1,2,0:T(8,128)(2,1)}, bf16[2,512,512]{2,1,0:T(8,128)(2,1)}, bf16[2,512,512]{1,2,0:T(8,128)(2,1)}, bf16[2,512,8,64]{...) while((s32[]{:T(128)}, bf16[2,512,512]{1,2,0:T(8,128)(2,1)}, ...), condition=%wide.region_17.18_spmd, body=%wide.region_15.17_spmd.sunk | while | flops 1374941184 | bytes 89248512 | solution.py:160
  393.7 7.7 convert_bitcast_fusion
  401.4 7.7 copy.83
  409.1 4.8 convolution_convert_fusion.5
  414.0 10.2 %convolution_convert_fusion = bf16[2048,1024]{0,1:T(8,128)(2,1)} fusion(bf16[1024,2048]{1,0:T(8,128)(2,1)} %copy-done.40, f32[1024,1024]{1,0:T(8,128)} %copy-done.11), kind=kOutput, calls=%fused_computation.91 | convolution fusion | flops 4298113024 | bytes 12582912 | tf_op jit(solution)/shard_map/dot_general | solution.py:22
  424.3 6.6 bitcast_convert_fusion
  431.3 10.2 %convolution_convert_fusion.1 = bf16[1024,2048]{1,0:T(8,128)(2,1)} fusion(bf16[1024,2048]{1,0:T(8,128)(2,1)} %get-tuple-element.277, f32[1024,1024]{1,0:T(8,128)} %copy-done.7, f32[1024]{0:T(1024)S(1)} %copy-done.25, f32[1024]{0:T(1024)S(1)} %convert_element_type.169), kind=kOutput, calls=%fused_computation.92 | convolution fusion | flops 4300210176 | bytes 12591104 | tf_op jit(solution)/shard_map/dot_general | solution.py:22
  452.0 68.8 %all-reduce.13.cloned.1.call-done = bf16[3,1024,512]{2,0,1:T(4,128)(2,1)} async-done(((bf16[3,1024,512]{2,0,1:T(4,128)(2,1)}), bf16[3,1024,512]{2,0,1:T(4,128)(2,1)}) %all-reduce.13.cloned.1.call-update) | async-done | bytes 3145744
  522.7 57.9 %reduce-scatter.7.cloned.1.call-done = bf16[512,64]{0,1:T(8,128)(2,1)} async-done(((bf16[512,1024]{0,1:T(8,128)(2,1)}), bf16[512,64]{0,1:T(8,128)(2,1)}) %reduce-scatter.7.cloned.1.call-update) | async-done | bytes 65552 | tf_op jit(solution)/shard_map/reduce_scatter | solution.py:185
  582.1 74.2 %reduce-scatter.11.cloned.1.call-done = bf16[2048,64]{0,1:T(8,128)(2,1)} async-done(((bf16[2048,1024]{0,1:T(8,128)(2,1)}), bf16[2048,64]{0,1:T(8,128)(2,1)}) %reduce-scatter.11.cloned.1.call-update) | async-done | bytes 262160 | tf_op jit(solution)/shard_map/reduce_scatter | solution.py:191
  658.1 31.3 %reduce-scatter.5.cloned.1.call-done = bf16[512,1024]{1,0:T(8,128)(2,1)} async-done(((bf16[1024,1024]{1,0:T(8,128)(2,1)}), bf16[512,1024]{1,0:T(8,128)(2,1)}) %reduce-scatter.5.cloned.1.call-update) | async-done | bytes 1048592 | tf_op jit(solution)/shard_map/reduce_scatter | solution.py:179
  692.6 40.9 %all-reduce.1 = (f32[2,1024]{1,0:T(2,128)}, f32[1024]{0:T(1024)}, f32[1024]{0:T(1024)}, f32[1024]{0:T(1024)}, f32[4096]{0:T(1024)}, /*index=5*/f32[1024]{0:T(1024)}, f32[1024]{0:T(1024)}, f32[1024]{0:T(1024)}) all-reduce(f32[2,1024]{1,0:T(2,128)S(1)} %maximum_dynamic-update-slice_fusion, ...), channel_id=1, replica_groups=mesh['dp'=16,'mp'=2] {'dp','mp'}, use_global_device_ids=true, to_apply=%region_22.23 | all-reduce | flops 12288 | bytes 98304 | tf_op jit(solution)/shard_map/psum | solution.py:201
  733.5 33.2 %reduce-scatter.9.cloned.1.call-done = bf16[64,2048]{1,0:T(8,128)(2,1)} async-done(((bf16[1024,2048]{1,0:T(8,128)(2,1)}), bf16[64,2048]{1,0:T(8,128)(2,1)}) %reduce-scatter.9.cloned.1.call-update) | async-done | bytes 262160 | tf_op jit(solution)/shard_map/reduce_scatter | solution.py:188
  (204 shorter events, 148.5 us)
Async XLA Ops:
  7.2 119.5 %all-reduce.7.cloned.1.call-start = ((), (), s32[]{:S(2)}) async-start(), calls=%async_computation.4 | async-start | bytes 4194304 | tf_op jit(solution)/shard_map/psum | solution.py:119
  56.7 4.6 copy-start.27
  60.9 167.8 %all-reduce.9.cloned.1.call-start = ((), (), s32[]{:S(2)}) async-start(), calls=%async_computation.5 | async-start | bytes 4194304 | tf_op jit(solution)/shard_map/psum | solution.py:132
  61.3 171.4 %copy-start.24 = (f32[1024]{0:T(1024)}, f32[1024]{0:T(1024)S(1)}, u32[]{:S(2)}) copy-start(f32[1024]{0:T(1024)S(1)} %convert_element_type.170) | copy-start | bytes 12292
  133.4 24.4 %copy-start.7 = (f32[1024,1024]{1,0:T(8,128)}, f32[1024,1024]{1,0:T(8,128)S(1)}, u32[]{:S(2)}) copy-start(f32[1024,1024]{1,0:T(8,128)S(1)} %broadcast_multiply_fusion) | copy-start | bytes 12582916
  133.5 26.5 %copy-start.34 = (bf16[2048,1024]{1,0:T(8,128)(2,1)S(1)}, bf16[2048,1024]{1,0:T(8,128)(2,1)}, u32[]{:S(2)}) copy-start(bf16[2048,1024]{1,0:T(8,128)(2,1)} %param.29) | copy-start | bytes 12582916
  159.9 6.2 copy-start.31
  159.9 6.2 copy-start.32
  165.7 159.5 %all-reduce.11.cloned.1.call-start = ((), (), s32[]{:S(2)}) async-start(), calls=%async_computation.6 | async-start | bytes 4194304 | tf_op jit(solution)/shard_map/psum | solution.py:149
  166.2 72.0 %copy-start.20 = (f32[1024]{0:T(1024)}, f32[1024]{0:T(1024)S(1)}, u32[]{:S(2)}) copy-start(f32[1024]{0:T(1024)S(1)} %convert_element_type.177) | copy-start | bytes 12292
  228.8 4.7 copy-start.13
  239.4 14.7 %copy-start.11 = (f32[1024,1024]{1,0:T(8,128)}, f32[1024,1024]{1,0:T(8,128)S(1)}, u32[]{:S(2)}) copy-start(f32[1024,1024]{1,0:T(8,128)S(1)} %broadcast_add_fusion.1) | copy-start | bytes 12582916
  241.1 13.0 %copy-start.37 = (bf16[1024,2048]{1,0:T(8,128)(2,1)S(1)}, bf16[1024,2048]{1,0:T(8,128)(2,1)}, u32[]{:S(2)}) copy-start(bf16[1024,2048]{1,0:T(8,128)(2,1)} %param.27) | copy-start | bytes 12582916
  262.1 258.7 %all-reduce.13.cloned.1.call-start = ((), (), s32[]{:S(2)}) async-start(), calls=%async_computation.11 | async-start | bytes 8388608
  325.2 5.8 copy-start.4
  325.2 5.8 copy-start.6
  409.1 171.5 %reduce-scatter.7.cloned.1.call-start = ((), (), s32[]{:S(2)}) async-start(), calls=%async_computation.8 | async-start | bytes 1114112 | tf_op jit(solution)/shard_map/reduce_scatter | solution.py:185
  414.0 242.3 %reduce-scatter.11.cloned.1.call-start = ((), (), s32[]{:S(2)}) async-start(), calls=%async_computation.10 | async-start | bytes 4456448 | tf_op jit(solution)/shard_map/reduce_scatter | solution.py:191
  424.3 7.0 copy-start.25
  424.3 265.1 %reduce-scatter.5.cloned.1.call-start = ((), (), s32[]{:S(2)}) async-start(), calls=%async_computation.7 | async-start | bytes 3145728 | tf_op jit(solution)/shard_map/reduce_scatter | solution.py:179
  431.0 335.8 %reduce-scatter.9.cloned.1.call-start = ((), (), s32[]{:S(2)}) async-start(), calls=%async_computation.9 | async-start | bytes 4456448 | tf_op jit(solution)/shard_map/reduce_scatter | solution.py:188
  443.4 6.0 copy-start.9
  445.8 5.8 copy-start.18
  445.8 5.8 copy-start.19
  (30 other events, 79.6 us)
Sparse Core Ops, SparseCore 0:
  61.1 65.5 all-reduce.6
  165.8 62.9 all-reduce.8
  262.2 62.9 all-reduce.10
  409.2 111.5 all-reduce.12
  524.3 56.2 reduce-scatter.6
  584.8 71.4 reduce-scatter.10
  658.5 30.8 reduce-scatter.4
  693.8 72.9 reduce-scatter.8
where the time goes:
time: 785 us; the launch traced here: 776 us
  waiting for transfers between devices  457 us (58%)
  matrix products  139 us (18%)
  local copies, waits for them, and re-layouts  70.2 us (9%)
  other arithmetic  51.3 us (7%)
  blocking collectives  40.9 us (5%)
  between operations  15.7 us (2%)
    reduce_scatter x1, waiting for transfers between devices, local(): lax.psum_scatter(dff2_weight.astype(jnp.bfloat16), 'dp', scatter_dimensio...  74.2 us
    unnamed x9, waiting for transfers between devices  68.9 us
    psum x1, waiting for transfers between devices, local(): attn = lax.psum(attn_part, 'mp').astype(jnp.float32)  65.4 us
    psum x1, waiting for transfers between devices, local(): dhidden = dsecond + lax.psum(dhid_part, 'mp').astype(jnp.float32)  63 us
    psum x1, waiting for transfers between devices, local(): ffn = lax.psum(ffn_part, 'mp').astype(jnp.float32)  62.6 us
    reduce_scatter x1, waiting for transfers between devices, local(): lax.psum_scatter(dout_weight.astype(jnp.bfloat16), 'dp', scatter_dimensio...  57.9 us
    psum x1, blocking collectives, local(): lax.psum((qv_placed, dout_bias, dgain_one, dshift_one, ff1_placed, dff2_b...  40.9 us
    reduce_scatter x1, waiting for transfers between devices, local(): lax.psum_scatter(dff1_weight.astype(jnp.bfloat16), 'dp', scatter_dimensio...  33.2 us
  transfers between devices with their start and end apart: 8, of which 8 were waited for; matrix products, arithmetic and copies ran while one was open for 6% of the time, Pallas kernels for 0%

commit v1 on v0

--- a/solution.py
+++ b/solution.py
@@ -146,7 +146,7 @@
     dff1_bias = jnp.sum(dpre.astype(jnp.float32), axis=0)
     dff1_weight = over_rows(hidden_low, dpre)
     dhid_part = over_cols(dpre, ff1_weight).astype(jnp.bfloat16)
-    dhidden = dsecond + lax.psum(dhid_part, "mp").astype(jnp.float32)
+    dhidden = dsecond + jnp.sum(lax.all_gather(dhid_part, "mp"), axis=0).astype(jnp.float32)
     dfirst = norm_one_back(dhidden * gain_one)[0]
     dattn = dfirst.astype(jnp.bfloat16)
     dhidden_own = own_rows(dhidden)

time: 785 us -> 825 us (1.051)
  waiting for transfers between devices: 457 us -> 492 us
    psum x1 -> x0, waiting for transfers between devices: 63 us -> none  [local(): dhidden = dsecond + lax.psum(dhid_part, 'mp').astype(jnp.float32)]
    all_gather x0 -> x1, waiting for transfers between devices: none -> 56.9 us  [local(): lax.all_gather(dhid_part, 'mp')]
    reduce_scatter x1, waiting for transfers between devices: 33.2 us -> 74 us  [local(): lax.psum_scatter(dff1_weight.astype(jnp.bfloat16), 'dp', scatter_dimensio...]
where the time goes in v1:
time: 825 us; the launch traced here: 816 us
  waiting for transfers between devices  492 us (60%)
  matrix products  139 us (17%)
  local copies, waits for them, and re-layouts  69.9 us (8%)
  other arithmetic  56.4 us (7%)
  blocking collectives  40.7 us (5%)
  between operations  15.8 us (2%)
    reduce_scatter x1, waiting for transfers between devices, local(): lax.psum_scatter(dff1_weight.astype(jnp.bfloat16), 'dp', scatter_dimensio...  74 us
    reduce_scatter x1, waiting for transfers between devices, local(): lax.psum_scatter(dff2_weight.astype(jnp.bfloat16), 'dp', scatter_dimensio...  73.9 us
    unnamed x9, waiting for transfers between devices  69.2 us
    psum x1, waiting for transfers between devices, local(): attn = lax.psum(attn_part, 'mp').astype(jnp.float32)  65.4 us
    psum x1, waiting for transfers between devices, local(): ffn = lax.psum(ffn_part, 'mp').astype(jnp.float32)  62.6 us
    reduce_scatter x1, waiting for transfers between devices, local(): lax.psum_scatter(dout_weight.astype(jnp.bfloat16), 'dp', scatter_dimensio...  58.4 us
    all_gather x1, waiting for transfers between devices, local(): lax.all_gather(dhid_part, 'mp')  56.9 us
    psum x1, blocking collectives, local(): lax.psum((qv_placed, dout_bias, dgain_one, dshift_one, ff1_placed, dff2_b...  40.7 us
  transfers between devices with their start and end apart: 8, of which 8 were waited for; matrix products, arithmetic and copies ran while one was open for 6% of the time, Pallas kernels for 0%

profile of v1, /device:TPU:0, one launch (start us, length us, event | category | flops | bytes accessed | tf_op | source)
XLA Modules:
  0.0 815.7 jit_solution(12681454612687802865)
XLA Ops:
  9.1 5.5 fusion.56
  32.4 24.3 %while.26 = (s32[]{:T(128)}, bf16[2,512,512]{2,1,0:T(8,128)(2,1)}, f32[2,8,512]{2,1,0:T(8,128)S(1)}, bf16[2,512,8,64]{1,3,2,0:T(8,128)(2,1)}, pred[2,512]{1,0:T(...) while((s32[]{:T(128)}, bf16[2,512,512]{2,1,0:T(8,128)(2,1)}, ...), condition=%wide.region_3.4_spmd, body=%wide.region_0.3_spmd.sunk | while | flops 562294784 | bytes 33689224 | solution.py:114
  61.3 65.4 %all-reduce.6.cloned.1.call-done = bf16[1024,1024]{1,0:T(8,128)(2,1)} async-done(((bf16[1024,1024]{1,0:T(8,128)(2,1)}), bf16[1024,1024]{1,0:T(8,128)(2,1)}) %all-reduce.6.cloned.1.call-update) | async-done | bytes 2097168 | tf_op jit(solution)/shard_map/psum | solution.py:119
  133.5 24.4 %multiply_convert_fusion.1 = (bf16[1024,2048]{1,0:T(8,128)(2,1)S(1)}, f32[1024,2048]{1,0:T(8,128)}, f32[1024,2048]{1,0:T(8,128)}) fusion(f32[2048]{0:T(1024)S(1)} %convert_element_type.174, bf16[1024,2048]{1,0:T(8,128)(2,1)S(1)} %copy-done.36, f32[1024,1024]{1,0:T(8,128)S(1)} %broadcast_multiply_fusion, f32[1024]{0:T(1024)S(1)} %convert_element_type.172, ...), kind=kOutput, calls=%fused_computation.64 | convolution fusion | flops 4436525056 | bytes 29376512 | tf_op jit(solution)/shard_map/dot_general | solution.py:125
  159.8 5.8 convolution_convert_fusion.3
  166.1 62.6 %all-reduce.8.cloned.1.call-done = bf16[1024,1024]{1,0:T(8,128)(2,1)} async-done(((bf16[1024,1024]{1,0:T(8,128)(2,1)}), bf16[1024,1024]{1,0:T(8,128)(2,1)}) %all-reduce.8.cloned.1.call-update) | async-done | bytes 2097168 | tf_op jit(solution)/shard_map/psum | solution.py:132
  241.1 13.0 %convert_reduce_fusion = (f32[2048]{0:T(1024)}, bf16[1024,2048]{1,0:T(8,128)(2,1)}) fusion(f32[1024,2048]{1,0:T(8,128)} %get-tuple-element.258, bf16[2048,1024]{1,0:T(8,128)(2,1)S(1)} %copy-done.35, f32[1024,1024]{1,0:T(8,128)S(1)} %broadcast_add_fusion.1, f32[1024,2048]{1,0:T(8,128)} %get-tuple-element.275, f32[2048]{0:T(1024)S(1)} %convert_element_type.174), kind=kOutput, calls=%fused_computation.62 | convolution fusion | flops 4331665408 | bytes 29376512 | tf_op jit(solution)/shard_map/dot_general | solution.py:28
  254.1 8.0 convolution_convert_fusion.2
  262.2 56.9 %all-gather.3.cloned.1.call-done = bf16[2048,1024]{1,0:T(8,128)(2,1)} async-done(((bf16[1024,1024]{1,0:T(8,128)(2,1)}), bf16[2048,1024]{1,0:T(8,128)(2,1)}) %all-gather.3.cloned.1.call-update) | async-done | bytes 4194320 | tf_op jit(solution)/shard_map/all_gather | solution.py:149
  319.1 5.2 reduce_sum.205
  324.2 5.7 multiply_reduce_fusion.1
  345.3 42.9 %while.27 = (s32[]{:T(128)}, bf16[2,512,512]{1,2,0:T(8,128)(2,1)}, bf16[2,512,512]{2,1,0:T(8,128)(2,1)}, bf16[2,512,512]{1,2,0:T(8,128)(2,1)}, bf16[2,512,8,64]{...) while((s32[]{:T(128)}, bf16[2,512,512]{1,2,0:T(8,128)(2,1)}, ...), condition=%wide.region_17.18_spmd, body=%wide.region_15.17_spmd.sunk | while | flops 1374941184 | bytes 89248512 | solution.py:160
  392.7 7.7 convert_bitcast_fusion
  400.5 7.7 copy.83
  408.2 4.8 convolution_convert_fusion.5
  413.1 10.2 %convolution_convert_fusion = bf16[2048,1024]{0,1:T(8,128)(2,1)} fusion(bf16[1024,2048]{1,0:T(8,128)(2,1)} %copy-done.40, f32[1024,1024]{1,0:T(8,128)} %copy-done.11), kind=kOutput, calls=%fused_computation.91 | convolution fusion | flops 4298113024 | bytes 12582912 | tf_op jit(solution)/shard_map/dot_general | solution.py:22
  424.0 10.1 %convolution_convert_fusion.1 = bf16[1024,2048]{1,0:T(8,128)(2,1)} fusion(bf16[1024,2048]{1,0:T(8,128)(2,1)} %get-tuple-element.277, f32[1024,1024]{1,0:T(8,128)} %copy-done.7, f32[1024]{0:T(1024)S(1)} %copy-done.25, f32[1024]{0:T(1024)S(1)} %convert_element_type.171), kind=kOutput, calls=%fused_computation.92 | convolution fusion | flops 4300210176 | bytes 12591104 | tf_op jit(solution)/shard_map/dot_general | solution.py:22
  434.2 6.6 bitcast_convert_fusion
  450.7 69.1 %all-reduce.10.cloned.1.call-done = bf16[3,1024,512]{2,0,1:T(4,128)(2,1)} async-done(((bf16[3,1024,512]{2,0,1:T(4,128)(2,1)}), bf16[3,1024,512]{2,0,1:T(4,128)(2,1)}) %all-reduce.10.cloned.1.call-update) | async-done | bytes 3145744
  521.6 58.4 %reduce-scatter.7.cloned.1.call-done = bf16[512,64]{0,1:T(8,128)(2,1)} async-done(((bf16[512,1024]{0,1:T(8,128)(2,1)}), bf16[512,64]{0,1:T(8,128)(2,1)}) %reduce-scatter.7.cloned.1.call-update) | async-done | bytes 65552 | tf_op jit(solution)/shard_map/reduce_scatter | solution.py:185
  581.5 73.9 %reduce-scatter.11.cloned.1.call-done = bf16[2048,64]{0,1:T(8,128)(2,1)} async-done(((bf16[2048,1024]{0,1:T(8,128)(2,1)}), bf16[2048,64]{0,1:T(8,128)(2,1)}) %reduce-scatter.11.cloned.1.call-update) | async-done | bytes 262160 | tf_op jit(solution)/shard_map/reduce_scatter | solution.py:191
  657.3 74.0 %reduce-scatter.9.cloned.1.call-done = bf16[64,2048]{1,0:T(8,128)(2,1)} async-done(((bf16[1024,2048]{1,0:T(8,128)(2,1)}), bf16[64,2048]{1,0:T(8,128)(2,1)}) %reduce-scatter.9.cloned.1.call-update) | async-done | bytes 262160 | tf_op jit(solution)/shard_map/reduce_scatter | solution.py:188
  733.0 31.4 %reduce-scatter.5.cloned.1.call-done = bf16[512,1024]{1,0:T(8,128)(2,1)} async-done(((bf16[1024,1024]{1,0:T(8,128)(2,1)}), bf16[512,1024]{1,0:T(8,128)(2,1)}) %reduce-scatter.5.cloned.1.call-update) | async-done | bytes 1048592 | tf_op jit(solution)/shard_map/reduce_scatter | solution.py:179
  767.7 40.7 %all-reduce.1 = (f32[2,1024]{1,0:T(2,128)}, f32[1024]{0:T(1024)}, f32[1024]{0:T(1024)}, f32[1024]{0:T(1024)}, f32[4096]{0:T(1024)}, /*index=5*/f32[1024]{0:T(1024)}, f32[1024]{0:T(1024)}, f32[1024]{0:T(1024)}) all-reduce(f32[2,1024]{1,0:T(2,128)S(1)} %maximum_dynamic-update-slice_fusion, ...), channel_id=1, replica_groups=mesh['dp'=16,'mp'=2] {'dp','mp'}, use_global_device_ids=true, to_apply=%region_22.23 | all-reduce | flops 12288 | bytes 98304 | tf_op jit(solution)/shard_map/psum | solution.py:201
  (205 shorter events, 152.3 us)
Async XLA Ops:
  7.2 119.5 %all-reduce.6.cloned.1.call-start = ((), (), s32[]{:S(2)}) async-start(), calls=%async_computation.4 | async-start | bytes 4194304 | tf_op jit(solution)/shard_map/psum | solution.py:119
  60.9 167.8 %all-reduce.8.cloned.1.call-start = ((), (), s32[]{:S(2)}) async-start(), calls=%async_computation.5 | async-start | bytes 4194304 | tf_op jit(solution)/shard_map/psum | solution.py:132
  61.3 171.3 %copy-start.24 = (f32[1024]{0:T(1024)}, f32[1024]{0:T(1024)S(1)}, u32[]{:S(2)}) copy-start(f32[1024]{0:T(1024)S(1)} %convert_element_type.172) | copy-start | bytes 12292
  133.4 24.4 %copy-start.7 = (f32[1024,1024]{1,0:T(8,128)}, f32[1024,1024]{1,0:T(8,128)S(1)}, u32[]{:S(2)}) copy-start(f32[1024,1024]{1,0:T(8,128)S(1)} %broadcast_multiply_fusion) | copy-start | bytes 12582916
  133.5 26.4 %copy-start.34 = (bf16[2048,1024]{1,0:T(8,128)(2,1)S(1)}, bf16[2048,1024]{1,0:T(8,128)(2,1)}, u32[]{:S(2)}) copy-start(bf16[2048,1024]{1,0:T(8,128)(2,1)} %param.29) | copy-start | bytes 12582916
  159.8 6.3 copy-start.31
  159.8 6.3 copy-start.32
  165.6 153.4 %all-gather.3.cloned.1.call-start = ((), (), s32[]{:S(2)}) async-start(), calls=%async_computation.10 | async-start | bytes 6291456 | tf_op jit(solution)/shard_map/all_gather | solution.py:149
  166.1 72.0 %copy-start.20 = (f32[1024]{0:T(1024)}, f32[1024]{0:T(1024)S(1)}, u32[]{:S(2)}) copy-start(f32[1024]{0:T(1024)S(1)} %convert_element_type.179) | copy-start | bytes 12292
  239.4 14.7 %copy-start.11 = (f32[1024,1024]{1,0:T(8,128)}, f32[1024,1024]{1,0:T(8,128)S(1)}, u32[]{:S(2)}) copy-start(f32[1024,1024]{1,0:T(8,128)S(1)} %broadcast_add_fusion.1) | copy-start | bytes 12582916
  241.1 13.0 %copy-start.37 = (bf16[1024,2048]{1,0:T(8,128)(2,1)S(1)}, bf16[1024,2048]{1,0:T(8,128)(2,1)}, u32[]{:S(2)}) copy-start(bf16[1024,2048]{1,0:T(8,128)(2,1)} %param.27) | copy-start | bytes 12582916
  262.1 257.7 %all-reduce.10.cloned.1.call-start = ((), (), s32[]{:S(2)}) async-start(), calls=%async_computation.11 | async-start | bytes 8388608
  324.2 5.8 copy-start.4
  324.2 5.8 copy-start.6
  408.2 171.9 %reduce-scatter.7.cloned.1.call-start = ((), (), s32[]{:S(2)}) async-start(), calls=%async_computation.7 | async-start | bytes 1114112 | tf_op jit(solution)/shard_map/reduce_scatter | solution.py:185
  413.0 242.4 %reduce-scatter.11.cloned.1.call-start = ((), (), s32[]{:S(2)}) async-start(), calls=%async_computation.9 | async-start | bytes 4456448 | tf_op jit(solution)/shard_map/reduce_scatter | solution.py:191
  423.3 307.9 %reduce-scatter.9.cloned.1.call-start = ((), (), s32[]{:S(2)}) async-start(), calls=%async_computation.8 | async-start | bytes 4456448 | tf_op jit(solution)/shard_map/reduce_scatter | solution.py:188
  434.2 6.8 copy-start.33
  434.2 6.8 copy-start.39
  434.2 8.0 copy-start.23
  434.2 8.1 copy-start.26
  434.2 330.3 %reduce-scatter.5.cloned.1.call-start = ((), (), s32[]{:S(2)}) async-start(), calls=%async_computation.6 | async-start | bytes 3145728 | tf_op jit(solution)/shard_map/reduce_scatter | solution.py:179
  442.2 6.0 copy-start.9
  444.6 5.7 copy-start.18
  (30 other events, 89.3 us)
Sparse Core Ops, SparseCore 0:
  61.1 65.5 all-reduce.5
  165.8 62.9 all-reduce.7
  262.3 56.7 all-gather.2
  408.3 111.4 all-reduce.9
  523.7 56.3 reduce-scatter.6
  583.8 71.6 reduce-scatter.10
  659.8 71.3 reduce-scatter.8
  733.5 30.9 reduce-scatter.4
